TPU v7x, 512 devices: a whole 4x8x8 slice. The times are simulated.
512 devices in a mesh: depth: 4 (over x), row: 8 (over z_hi, core), col: 16 (over z_lo, y).
Axes of the slice: x: 4, y: 8, z: 8 (z_hi: 4, z_lo: 2; z = z_hi * 2 + z_lo), core: 2. Of those that a mesh axis runs over, the one named last changes fastest.
Arguments:
- tokens: bfloat16 [512, 6144], P(('depth', 'row'), 'col'), may hold values from -6 to 6
- grad_out: bfloat16 [512, 6144], P(('depth', 'row'), 'col'), may hold values from -6 to 6
- w_up: bfloat16 [6144, 24576], P(('col', 'depth'), 'row'), may hold values from -0.078125 to 0.078125
- w_down: bfloat16 [6144, 24576], P(('col', 'depth'), 'row'), may hold values from -0.0390625 to 0.0390625
Outputs:
- grad_in: bfloat16 [512, 6144], P(('depth', 'row'), 'col')
- grad_up: bfloat16 [6144, 24576], P(('col', 'depth'), 'row')
- grad_down: bfloat16 [6144, 24576], P(('col', 'depth'), 'row')
All inputs are finite; a program needn't handle non-finite values.
Results may differ from a plain program's by a relative error of at most 0.03.
Values may be sent and summed in bfloat16 or wider, within the bound.
No kernel may reach another device: no remote copies, remote signals or barrier semaphores. Data moves between devices by JAX's collectives and lax.ppermute only.
A program may use at most 64 MiB of HBM per device.

v0:
```python
import math
import jax
import jax.numpy as jnp
from jax import lax
from jax.sharding import PartitionSpec as P


def gelu_parts(hidden):
    coeff = math.sqrt(2.0 / math.pi)
    cube = hidden * hidden * hidden
    slope_in = jnp.tanh(coeff * (hidden + 0.044715 * cube))
    value = 0.5 * hidden * (1.0 + slope_in)
    slope = 0.5 * (1.0 + slope_in) + 0.5 * hidden * (1.0 - slope_in * slope_in) * coeff * (
        1.0 + 3.0 * 0.044715 * hidden * hidden
    )
    return (value, slope)


def body(tokens, grad_out, w_up, w_down):
    depth_pos = lax.axis_index("depth")
    up_block, down_block = (
        lax.all_gather(w_up, "depth", axis=0, tiled=True),
        lax.all_gather(w_down, "depth", axis=0, tiled=True),
    )
    x_rows, dy_rows = (
        lax.all_gather(tokens, ("depth", "row"), axis=0, tiled=True),
        lax.all_gather(grad_out, ("depth", "row"), axis=0, tiled=True),
    )
    own_count = x_rows.shape[0] // lax.axis_size("depth")
    own_start = depth_pos * own_count
    x_own = lax.dynamic_slice_in_dim(x_rows, own_start, own_count, 0)
    dy_own = lax.dynamic_slice_in_dim(dy_rows, own_start, own_count, 0)
    narrow = w_up.shape[0]
    dy_narrow = lax.dynamic_slice_in_dim(dy_rows, depth_pos * narrow, narrow, 1)
    pre_part = jnp.dot(x_rows, up_block, preferred_element_type=jnp.float32)
    grad_part = jnp.dot(dy_own, down_block, preferred_element_type=jnp.float32)
    hidden_pre, act_grad = (
        lax.psum(pre_part.astype(jnp.bfloat16), "col").astype(jnp.float32),
        lax.psum(grad_part.astype(jnp.bfloat16), "col").astype(jnp.float32),
    )
    act_value, slope = gelu_parts(hidden_pre)
    act_rows = act_value.astype(jnp.bfloat16)
    slope_own = lax.dynamic_slice_in_dim(slope, own_start, own_count, 0)
    hidden_grad = (act_grad * slope_own).astype(jnp.bfloat16)
    grad_up = lax.psum_scatter(
        lax.dot_general(
            x_own, hidden_grad, (((0,), (0,)), ((), ())), preferred_element_type=jnp.float32
        ).astype(jnp.bfloat16),
        "depth",
        scatter_dimension=0,
        tiled=True,
    )
    grad_in = lax.psum_scatter(
        lax.dot_general(
            hidden_grad, up_block, (((1,), (1,)), ((), ())), preferred_element_type=jnp.float32
        ).astype(jnp.bfloat16),
        "row",
        scatter_dimension=0,
        tiled=True,
    )
    grad_down = lax.dot_general(
        dy_narrow, act_rows, (((0,), (0,)), ((), ())), preferred_element_type=jnp.float32
    ).astype(jnp.bfloat16)
    return (grad_in, grad_up, grad_down)


def solution(mesh):
    placed = (
        P(("depth", "row"), "col"),
        P(("depth", "row"), "col"),
        P(("col", "depth"), "row"),
        P(("col", "depth"), "row"),
    )
    return jax.shard_map(
        body,
        mesh=mesh,
        in_specs=placed,
        out_specs=(
            P(("depth", "row"), "col"),
            P(("col", "depth"), "row"),
            P(("col", "depth"), "row"),
        ),
        check_vma=False,
    )
```

profile of v0, /device:TPU:1, one launch (start us, length us, event | category | flops | bytes accessed | tf_op | source)
XLA Modules:
  0.0 356.0 jit_solution(12280223903495737786)
XLA Ops:
  7.2 0.0 all-gather.5.cloned.1.call-start
  7.2 0.7 all-gather.5.cloned.1.call-update
  7.9 0.0 all-gather.3.cloned.1.call-start
  7.9 0.7 all-gather.3.cloned.1.call-update
  8.6 0.0 all-reduce.3.cloned.1.call-start
  8.7 53.1 %all_gather.14 = bf16[512,384]{1,0:T(8,128)(2,1)S(1)} all-gather(bf16[16,384]{1,0:T(8,128)(2,1)} %param.4), channel_id=1, replica_groups=mesh['depth'=4,'row'=8,'col'=16] {'depth','row'}, dimensions={0}, use_global_device_ids=true | all-gather | bytes 405504 | tf_op jit(solution)/shard_map/all_gather | solution.py:26
  61.8 40.9 %all_gather.12 = bf16[512,384]{1,0:T(8,128)(2,1)S(1)} all-gather(bf16[16,384]{1,0:T(8,128)(2,1)} %param.5), channel_id=1, replica_groups=mesh['depth'=4,'row'=8,'col'=16] {'depth','row'}, dimensions={0}, use_global_device_ids=true | all-gather | bytes 405504 | tf_op jit(solution)/shard_map/all_gather | solution.py:27
  102.7 5.1 %convolution_convert_fusion = bf16[512,3072]{1,0:T(8,128)(2,1)} fusion(bf16[512,384]{1,0:T(8,128)(2,1)S(1)} %all_gather.14, bf16[384,3072]{1,0:T(8,128)(2,1)} %all-gather.5.cloned.1.call-done), kind=kOutput, calls=%fused_computation.6 | convolution fusion | flops 1209532416 | bytes 5898240 | tf_op jit(solution)/shard_map/dot_general | solution.py:35
  107.8 3.2 convolution_convert_fusion.2
  111.0 0.0 all-reduce.3.cloned.1.call-update
  111.0 0.0 reduce-scatter.3.cloned.1.call-start
  111.1 145.0 %all-reduce.3.cloned.1.call-done = (bf16[512,3072]{1,0:T(8,128)(2,1)}, bf16[128,3072]{1,0:T(8,128)(2,1)}) async-done(((bf16[512,3072]{1,0:T(8,128)(2,1)}, bf16[128,3072]{1,0:T(8,128)(2,1)}), (bf16[512,3072]{1,0:T(8,128)(2,1)}, bf16[128,3072]{1,0:T(8,128)(2,1)})) %all-reduce.3.cloned.1.call-update) | async-done | bytes 3932176 | tf_op jit(solution)/shard_map/psum | solution.py:38
  256.1 2.8 convert_element_type.30
  258.9 2.6 fusion.3
  261.5 0.7 fusion.8
  262.3 0.9 copy-done.1
  263.1 0.0 copy-done.2
  263.2 1.5 convolution_convert_fusion.4
  264.7 0.0 reduce-scatter.5.cloned.1.call-start
  264.7 3.4 convolution_convert_fusion.1
  268.1 0.0 reduce-scatter.5.cloned.1.call-update
  268.2 3.3 convolution_convert_fusion.3
  271.5 38.2 %reduce-scatter.3.cloned.1.call-done = bf16[16,384]{1,0:T(8,128)(2,1)} async-done(((bf16[128,384]{1,0:T(8,128)(2,1)}), bf16[16,384]{1,0:T(8,128)(2,1)}) %reduce-scatter.3.cloned.1.call-update) | async-done | bytes 12304 | tf_op jit(solution)/shard_map/reduce_scatter | solution.py:53
  309.7 39.8 %reduce-scatter.5.cloned.1.call-done = bf16[96,3072]{1,0:T(8,128)(2,1)} async-done(((bf16[384,3072]{1,0:T(8,128)(2,1)}), bf16[96,3072]{1,0:T(8,128)(2,1)}) %reduce-scatter.5.cloned.1.call-update) | async-done | bytes 589840 | tf_op jit(solution)/shard_map/reduce_scatter | solution.py:45
  (11 shorter events, 0.0 us)
Async XLA Ops:
  7.2 95.5 %all-gather.5.cloned.1.call-start = ((), (), s32[]{:S(2)}) async-start(), calls=%async_computation.3 | async-start | bytes 2949120 | tf_op jit(solution)/shard_map/all_gather | solution.py:22
  7.9 99.9 %all-gather.3.cloned.1.call-start = ((), (), s32[]{:S(2)}) async-start(), calls=%async_computation.2 | async-start | bytes 2949120 | tf_op jit(solution)/shard_map/all_gather | solution.py:23
  8.6 247.4 %all-reduce.3.cloned.1.call-start = ((), (), s32[]{:S(2)}) async-start(), calls=%async_computation.6 | async-start | bytes 7864320 | tf_op jit(solution)/shard_map/psum | solution.py:38
  61.8 46.0 %copy-start.4 = (bf16[512,384]{1,0:T(8,128)(2,1)}, bf16[512,384]{1,0:T(8,128)(2,1)S(1)}, u32[]{:S(2)}) copy-start(bf16[512,384]{1,0:T(8,128)(2,1)S(1)} %all_gather.14) | copy-start | bytes 1179652
  111.0 198.7 %reduce-scatter.3.cloned.1.call-start = ((), (), s32[]{:S(2)}) async-start(), calls=%async_computation.4 | async-start | bytes 110592 | tf_op jit(solution)/shard_map/reduce_scatter | solution.py:53
  256.1 2.9 copy-start
  258.9 2.6 copy-start.3
  261.5 1.7 copy-start.2
  262.2 0.9 copy-start.1
  264.7 84.8 %reduce-scatter.5.cloned.1.call-start = ((), (), s32[]{:S(2)}) async-start(), calls=%async_computation.5 | async-start | bytes 2949120 | tf_op jit(solution)/shard_map/reduce_scatter | solution.py:45
Sparse Core Ops, SparseCore 0:
  10.1 44.9 all-gather.4
  57.2 38.4 all-gather.2
  111.1 144.8 all-reduce.2
  264.8 44.8 reduce-scatter.2
  312.9 36.4 reduce-scatter.4
where the time goes:
time: 356 us
  waiting for transfers between devices  224 us (63%)
  blocking collectives  94 us (26%)
  matrix products  16.5 us (5%)
  between operations  13.9 us (4%)
  other arithmetic  6.11 us (2%)
    psum x1, waiting for transfers between devices, body(): lax.psum(pre_part.astype(jnp.bfloat16), 'col').astype(jnp.float32)  145 us
    all_gather x1, blocking collectives, body(): lax.all_gather(tokens, ('depth', 'row'), axis=0, tiled=True)  53.1 us
    all_gather x1, blocking collectives, body(): lax.all_gather(grad_out, ('depth', 'row'), axis=0, tiled=True)  40.9 us
    reduce_scatter x1, waiting for transfers between devices, body(): lax.psum_scatter(lax.dot_general(x_own, hidden_grad, (((0,), (0,)), ((),...  39.8 us
    reduce_scatter x1, waiting for transfers between devices, body(): lax.psum_scatter(lax.dot_general(hidden_grad, up_block, (((1,), (1,)), ((...  38.2 us
  transfers between devices with their start and end apart: 5, of which 3 were waited for; matrix products, arithmetic and copies ran while one was open for 3% of the time, Pallas kernels for 0%

commit v1 on v0

--- a/solution.py
+++ b/solution.py
@@ -23,7 +23,12 @@
         lax.all_gather(w_down, "depth", axis=0, tiled=True),
     )
     x_rows, dy_rows = (
-        lax.all_gather(tokens, ("depth", "row"), axis=0, tiled=True),
+        jnp.concatenate(
+            lax.all_to_all(
+                jnp.stack([tokens] * lax.axis_size(("depth", "row"))), ("depth", "row"), 0, 0
+            ),
+            axis=0,
+        ),
         lax.all_gather(grad_out, ("depth", "row"), axis=0, tiled=True),
     )
     own_count = x_rows.shape[0] // lax.axis_size("depth")

time: 356 us -> 349 us (0.980)
  blocking collectives: 94 us -> 50.2 us
  waiting for transfers between devices: 224 us -> 243 us
  starting transfers between devices: 0.2 us -> 14.6 us
    all_gather x1 -> x0, blocking collectives: 53.1 us -> none  [body(): lax.all_gather(tokens, ('depth', 'row'), axis=0, tiled=True)]
    all_gather x1, waiting for transfers between devices: 0.01 us -> 15.6 us  [body(): lax.all_gather(w_down, 'depth', axis=0, tiled=True)]
    all_to_all x0 -> x1, starting transfers between devices: none -> 14.4 us  [body(): lax.all_to_all(jnp.stack([tokens] * lax.axis_size(('depth', 'row'))), ('d...]
    all_gather x1, blocking collectives: 40.9 us -> 50.2 us  [body(): lax.all_gather(grad_out, ('depth', 'row'), axis=0, tiled=True)]
    psum x1, waiting for transfers between devices: 145 us -> 149 us  [body(): lax.psum(pre_part.astype(jnp.bfloat16), 'col').astype(jnp.float32)]
  transfers between devices with their start and end apart: 5 -> 6, of which waited for: 3 -> 4; matrix products, arithmetic and copies ran while one was open for 3% -> 4% of each run, Pallas kernels for 0% -> 0%
where the time goes in v1:
time: 349 us; the launch traced here: 348 us
  waiting for transfers between devices  243 us (70%)
  blocking collectives  50.2 us (14%)
  matrix products  17.6 us (5%)
  starting transfers between devices  14.6 us (4%)
  between operations  13.9 us (4%)
  other arithmetic  6.11 us (2%)
    psum x1, waiting for transfers between devices, body(): lax.psum(pre_part.astype(jnp.bfloat16), 'col').astype(jnp.float32)  149 us
    all_gather x1, blocking collectives, body(): lax.all_gather(grad_out, ('depth', 'row'), axis=0, tiled=True)  50.2 us
    reduce_scatter x1, waiting for transfers between devices, body(): lax.psum_scatter(lax.dot_general(x_own, hidden_grad, (((0,), (0,)), ((),...  39.8 us
    reduce_scatter x1, waiting for transfers between devices, body(): lax.psum_scatter(lax.dot_general(hidden_grad, up_block, (((1,), (1,)), ((...  37.3 us
    all_gather x1, waiting for transfers between devices, body(): lax.all_gather(w_down, 'depth', axis=0, tiled=True)  15.6 us
    all_to_all x1, starting transfers between devices, body(): lax.all_to_all(jnp.stack([tokens] * lax.axis_size(('depth', 'row'))), ('d...  14.4 us
  transfers between devices with their start and end apart: 6, of which 4 were waited for; matrix products, arithmetic and copies ran while one was open for 4% of the time, Pallas kernels for 0%

profile of v1, /device:TPU:1, one launch (start us, length us, event | category | flops | bytes accessed | tf_op | source)
XLA Modules:
  0.0 348.1 jit_solution(7975840372301254546)
XLA Ops:
  7.2 0.0 all-gather.5.cloned.1.call-start
  7.2 0.7 all-gather.5.cloned.1.call-update
  7.9 0.0 all-gather.3.cloned.1.call-start
  7.9 0.7 all-gather.3.cloned.1.call-update
  8.6 1.5 stack.2
  10.1 14.4 %all-to-all-start = ((bf16[32,16,384]{2,1,0:T(8,128)(2,1)}), bf16[32,16,384]{2,1,0:T(8,128)(2,1)S(1)}, u32[]{:S(2)}, u32[]{:S(2)}) async-start(bf16[32,16,384]{2,1,0:T(8,128)(2,1)} %stack.2), calls=%async_computation | async-start | bytes 786432 | tf_op jit(solution)/shard_map/all_to_all | solution.py:27
  24.6 0.0 all-reduce.3.cloned.1.call-start
  24.6 50.2 %all_gather.9 = bf16[512,384]{1,0:T(8,128)(2,1)S(1)} all-gather(bf16[16,384]{1,0:T(8,128)(2,1)} %param.5), channel_id=1, replica_groups=mesh['depth'=4,'row'=8,'col'=16] {'depth','row'}, dimensions={0}, use_global_device_ids=true | all-gather | bytes 405504 | tf_op jit(solution)/shard_map/all_gather | solution.py:32
  74.8 5.3 %convolution_convert_fusion = bf16[512,3072]{1,0:T(8,128)(2,1)} fusion(bf16[512,384]{1,0:T(8,128)(2,1)S(1)} %bitcast.7, bf16[384,3072]{1,0:T(8,128)(2,1)} %all-gather.5.cloned.1.call-done), kind=kOutput, calls=%fused_computation.6 | convolution fusion | flops 1209532416 | bytes 5898240 | tf_op jit(solution)/shard_map/dot_general | solution.py:40
  80.1 15.6 %all-gather.3.cloned.1.call-done = bf16[384,3072]{1,0:T(8,128)(2,1)} async-done(((bf16[96,3072]{1,0:T(8,128)(2,1)}), bf16[384,3072]{1,0:T(8,128)(2,1)}) %all-gather.3.cloned.1.call-update) | async-done | bytes 2359312 | tf_op jit(solution)/shard_map/all_gather | solution.py:23
  95.6 3.2 convolution_convert_fusion.2
  98.9 0.0 reduce-scatter.3.cloned.1.call-start
  98.9 149.2 %all-reduce.3.cloned.1.call-done = (bf16[512,3072]{1,0:T(8,128)(2,1)}, bf16[128,3072]{1,0:T(8,128)(2,1)}) async-done(((bf16[512,3072]{1,0:T(8,128)(2,1)}, bf16[128,3072]{1,0:T(8,128)(2,1)}), (bf16[512,3072]{1,0:T(8,128)(2,1)}, bf16[128,3072]{1,0:T(8,128)(2,1)})) %all-reduce.3.cloned.1.call-update) | async-done | bytes 3932176 | tf_op jit(solution)/shard_map/psum | solution.py:43
  248.2 2.8 convert_element_type.30
  251.0 2.6 fusion.3
  253.6 0.7 fusion.8
  254.3 0.9 copy-done.1
  255.2 0.0 copy-done.2
  255.3 1.5 convolution_convert_fusion.4
  256.8 0.0 reduce-scatter.5.cloned.1.call-start
  256.8 3.4 convolution_convert_fusion.1
  260.2 4.2 %convolution_convert_fusion.3 = bf16[96,3072]{1,0:T(8,128)(2,1)} fusion(bf16[512,3072]{1,0:T(8,128)(2,1)S(1)} %copy-done, bf16[512,384]{1,0:T(8,128)(2,1)} %copy-done.4, s32[]{:T(128)S(6)} %select_n.9), kind=kOutput, calls=%fused_computation.9 | convolution fusion | flops 318013440 | bytes 3866628 | tf_op jit(solution)/shard_map/dot_general | solution.py:66
  264.5 37.3 %reduce-scatter.3.cloned.1.call-done = bf16[16,384]{1,0:T(8,128)(2,1)} async-done(((bf16[128,384]{1,0:T(8,128)(2,1)}), bf16[16,384]{1,0:T(8,128)(2,1)}) %reduce-scatter.3.cloned.1.call-update) | async-done | bytes 12304 | tf_op jit(solution)/shard_map/reduce_scatter | solution.py:58
  301.8 39.8 %reduce-scatter.5.cloned.1.call-done = bf16[96,3072]{1,0:T(8,128)(2,1)} async-done(((bf16[384,3072]{1,0:T(8,128)(2,1)}), bf16[96,3072]{1,0:T(8,128)(2,1)}) %reduce-scatter.5.cloned.1.call-update) | async-done | bytes 589840 | tf_op jit(solution)/shard_map/reduce_scatter | solution.py:50
  (13 shorter events, 0.1 us)
Async XLA Ops:
  7.2 67.6 %all-gather.5.cloned.1.call-start = ((), (), s32[]{:S(2)}) async-start(), calls=%async_computation.4 | async-start | bytes 2949120 | tf_op jit(solution)/shard_map/all_gather | solution.py:22
  7.9 87.7 %all-gather.3.cloned.1.call-start = ((), (), s32[]{:S(2)}) async-start(), calls=%async_computation.3 | async-start | bytes 2949120 | tf_op jit(solution)/shard_map/all_gather | solution.py:23
  10.1 64.7 %all-to-all-start = ((bf16[32,16,384]{2,1,0:T(8,128)(2,1)}), bf16[32,16,384]{2,1,0:T(8,128)(2,1)S(1)}, u32[]{:S(2)}, u32[]{:S(2)}) async-start(bf16[32,16,384]{2,1,0:T(8,128)(2,1)} %stack.2), calls=%async_computation | async-start | bytes 786432 | tf_op jit(solution)/shard_map/all_to_all | solution.py:27
  24.6 223.6 %all-reduce.3.cloned.1.call-start = ((), (), s32[]{:S(2)}) async-start(), calls=%async_computation.7 | async-start | bytes 7864320 | tf_op jit(solution)/shard_map/psum | solution.py:43
  74.8 24.1 %copy-start.4 = (bf16[512,384]{1,0:T(8,128)(2,1)}, bf16[512,384]{1,0:T(8,128)(2,1)S(1)}, u32[]{:S(2)}) copy-start(bf16[512,384]{1,0:T(8,128)(2,1)S(1)} %all_gather.9) | copy-start | bytes 1179652
  98.9 202.9 %reduce-scatter.3.cloned.1.call-start = ((), (), s32[]{:S(2)}) async-start(), calls=%async_computation.5 | async-start | bytes 110592 | tf_op jit(solution)/shard_map/reduce_scatter | solution.py:58
  248.2 2.9 copy-start
  251.0 2.6 copy-start.3
  253.6 1.7 copy-start.2
  254.3 0.9 copy-start.1
  256.8 84.8 %reduce-scatter.5.cloned.1.call-start = ((), (), s32[]{:S(2)}) async-start(), calls=%async_computation.6 | async-start | bytes 2949120 | tf_op jit(solution)/shard_map/reduce_scatter | solution.py:50
Sparse Core Ops, SparseCore 0:
  10.1 46.4 all-gather.4
  58.7 36.9 all-gather.2
  99.0 149.1 all-reduce.2
  256.9 44.8 reduce-scatter.2
  305.1 36.4 reduce-scatter.4
